TPU v7x, 256 devices: a whole 4x4x8 slice. The times are simulated.
256 devices in a mesh: ens: 8 (over y, z_hi), tile: 32 (over z_lo, x, core).
Axes of the slice: x: 4, y: 4, z: 8 (z_hi: 2, z_lo: 4; z = z_hi * 4 + z_lo), core: 2. Of those that a mesh axis runs over, the one named last changes fastest.
Arguments:
- fields: bfloat16 [8, 32, 200, 8, 128], P('ens', 'tile'), may hold values from -6 to 6
- target: bfloat16 [8, 32, 200, 8, 128], P('ens', 'tile'), may hold values from -6 to 6
- wet_levels: int32 [32, 8, 128], P('tile'), may hold values from 0 to 19, as said below
- tile_links: int32 [32, 5], replicated, may hold values from -1 to 31, as said below
- tile_owner: int32 [32], replicated, may hold values from 0 to 31, as said below
- kernel: float32 [200, 49], replicated, may hold values from -0.875 to 0.875
- norm_gain: float32 [200], replicated, may hold values from 0.5 to 1.5
- weight_in: bfloat16 [200, 800], replicated, may hold values from -0.4375 to 0.4375
- weight_out: bfloat16 [800, 200], replicated, may hold values from -0.21875 to 0.21875
- layer_scale: float32 [200], replicated, may hold values from 0.25 to 1
Outputs:
- block_out: bfloat16 [8, 32, 200, 8, 128], P('ens', 'tile')
- grad_in: float32 [200, 800], replicated
- grad_out: float32 [800, 200], replicated
- grad_kernel: float32 [200, 49], replicated
Inputs may be any that keep to these rules, and one draw needn't show every extreme that they name: `wet_levels`: 0 is land; a cell is wet at the levels below its value. `tile_links`: the kept tiles are the kept blocks of a grid 8 tiles wide, numbered row by row from the south. West and east wrap around within a grid row; the southmost row has no south neighbour; the northmost row is complete, its north neighbour is the tile of the same row in the mirrored column 7 - column, and only it has flag 1 in column 4; -1 marks a missing neighbour. Column 4 is 0 or 1. `tile_owner`: a permutation.
All inputs are finite; a program needn't handle non-finite values.
Results may differ from a plain program's by a relative error of at most 0.005.
Values may be sent and summed in bfloat16 or wider, within the bound.
No kernel may reach another device: no remote copies, remote signals or barrier semaphores. Data moves between devices by JAX's collectives and lax.ppermute only.
A program may use at most 192 MiB of HBM per device.

v0:
```python
import jax
import jax.numpy as jnp
from jax import lax
from jax.sharding import PartitionSpec as P

LEVELS = 19
root_half = 0.7071067811865476
gauss_norm = 0.3989422804014327
norm_epsilon = 1e-06


def gelu_value(values):
    return 0.5 * values * (1.0 + lax.erf(values * root_half))


def gelu_slope(values):
    return (
        0.5 * (1.0 + lax.erf(values * root_half))
        + values * jnp.exp(-0.5 * values * values) * gauss_norm
    )


def take_slot(held, pieces, slot_id):
    piece_count = pieces.shape[0]
    inside = (slot_id >= 0) & (slot_id >= 0) & (slot_id < piece_count)
    taken = lax.dynamic_index_in_dim(
        pieces, jnp.clip(slot_id, 0, piece_count - 1), 0, keepdims=False
    )
    return jnp.where(inside, taken, held)


def local(
    fields,
    target,
    wet_levels,
    tile_links,
    tile_owner,
    kernel,
    norm_gain,
    weight_in,
    weight_out,
    layer_scale,
):
    members, _, channels, row_count, col_count = fields.shape
    tile_count = tile_owner.shape[0]
    own_slot = lax.axis_index("tile")
    own_tile = jnp.sum(
        jnp.where(tile_owner == own_slot, jnp.arange(tile_count, dtype=jnp.int32), 0)
    )
    level_of = jnp.arange(channels, dtype=jnp.int32) * LEVELS // channels
    wet_mask = wet_levels[0][None, :, :] > level_of[:, None, None]
    own_input = fields[:, 0]
    masked = jnp.where(wet_mask[None], own_input, jnp.zeros_like(own_input))
    entry_total = jnp.float32(
        members * lax.axis_size("ens") * tile_count * channels * row_count * col_count
    )

    def link_of(tile_id, column):
        return jnp.where(tile_id >= 0, tile_links[jnp.clip(tile_id, 0, tile_count - 1), column], -1)

    def slot_of(tile_id):
        return jnp.where(tile_id >= 0, tile_owner[jnp.clip(tile_id, 0, tile_count - 1)], -1)

    north_slot = slot_of(link_of(own_tile, 0))
    south_slot = slot_of(link_of(own_tile, 1))
    own_fold = link_of(own_tile, 4)
    west_tile = link_of(own_tile, 2)
    east_tile = link_of(own_tile, 3)
    west_slot = slot_of(west_tile)
    east_slot = slot_of(east_tile)
    zero_rows = jnp.zeros((members, channels, 3, col_count), jnp.bfloat16)
    row_strips = jnp.stack([masked[:, :, :3, :], masked[:, :, row_count - 3 :, :]], axis=0)[None]
    held = (zero_rows, zero_rows, zero_rows)
    pieces = lax.all_gather(row_strips, "tile", axis=0, tiled=True)
    lower_rows = take_slot(held[0], pieces[:, 0], north_slot)
    upper_rows = take_slot(held[1], pieces[:, 1], north_slot)
    below_rows = take_slot(held[2], pieces[:, 1], south_slot)
    north_rows = jnp.where(own_fold == 1, jnp.flip(upper_rows, (2, 3)), lower_rows)
    center = jnp.concatenate([below_rows, masked, north_rows], axis=2)
    side_cols = jnp.swapaxes(
        jnp.stack([center[..., :3], center[..., col_count - 3 :]], axis=0), 3, 4
    )[None]
    zero_cols = jnp.zeros((members, channels, 3, row_count + 6), jnp.bfloat16)
    held = (zero_cols, zero_cols)
    pieces = lax.all_gather(side_cols, "tile", axis=0, tiled=True)
    west_part = take_slot(held[0], pieces[:, 1], west_slot)
    east_part = take_slot(held[1], pieces[:, 0], east_slot)
    west_cols = jnp.swapaxes(west_part, 2, 3)
    east_cols = jnp.swapaxes(east_part, 2, 3)
    extended = jnp.concatenate([west_cols, center, east_cols], axis=3).astype(jnp.float32)
    conv_out = jnp.zeros((members, channels, row_count, col_count), jnp.float32)
    for row_off in range(7):
        for col_off in range(7):
            conv_out = (
                conv_out
                + kernel[:, 7 * row_off + col_off][None, :, None, None]
                * extended[:, :, row_off : row_off + row_count, col_off : col_off + col_count]
            )
    chan_mean = jnp.mean(conv_out, axis=1, keepdims=True)
    chan_var = jnp.mean((conv_out - chan_mean) ** 2, axis=1, keepdims=True)
    inv_std = 1.0 / jnp.sqrt(chan_var + norm_epsilon)
    centred = (conv_out - chan_mean) * inv_std
    gain_wide = norm_gain[None, :, None, None]
    scale_wide = layer_scale[None, :, None, None]
    normed = (centred * gain_wide).astype(jnp.bfloat16)
    flat_norm = normed.reshape(members, channels, row_count * col_count)
    hidden = jnp.einsum("ch,ecp->ehp", weight_in, flat_norm, preferred_element_type=jnp.float32)
    activated = gelu_value(hidden).astype(jnp.bfloat16)
    mlp_out = jnp.einsum("hc,ehp->ecp", weight_out, activated, preferred_element_type=jnp.float32)
    mlp_out = mlp_out.reshape(members, channels, row_count, col_count)
    block_out = (masked.astype(jnp.float32) + scale_wide * mlp_out).astype(jnp.bfloat16)
    misfit = jnp.where(
        wet_mask[None], block_out.astype(jnp.float32) - target[:, 0].astype(jnp.float32), 0.0
    )
    grad_mlp = (
        (2.0 * scale_wide * misfit)
        .astype(jnp.bfloat16)
        .reshape(members, channels, row_count * col_count)
    )
    part_out = jnp.einsum("ehp,ecp->hc", activated, grad_mlp, preferred_element_type=jnp.float32)
    grad_act = jnp.einsum("hc,ecp->ehp", weight_out, grad_mlp, preferred_element_type=jnp.float32)
    grad_hidden = (grad_act * gelu_slope(hidden)).astype(jnp.bfloat16)
    part_in = jnp.einsum("ecp,ehp->ch", flat_norm, grad_hidden, preferred_element_type=jnp.float32)
    grad_normed = jnp.einsum(
        "ch,ehp->ecp", weight_in, grad_hidden, preferred_element_type=jnp.float32
    )
    grad_scaled = grad_normed.reshape(members, channels, row_count, col_count) * gain_wide
    grad_conv = (
        grad_scaled
        - jnp.mean(grad_scaled, axis=1, keepdims=True)
        - centred * jnp.mean(grad_scaled * centred, axis=1, keepdims=True)
    ) * inv_std
    kernel_terms = []
    for row_off in range(7):
        for col_off in range(7):
            kernel_terms.append(
                jnp.sum(
                    grad_conv
                    * extended[:, :, row_off : row_off + row_count, col_off : col_off + col_count],
                    axis=(0, 2, 3),
                )
            )
    part_kernel = jnp.stack(kernel_terms, axis=1)
    sum_in, sum_out, sum_kernel = lax.psum((part_in, part_out, part_kernel), ("ens", "tile"))
    return (
        block_out[:, None],
        sum_in / entry_total,
        sum_out / entry_total,
        sum_kernel / entry_total,
    )


def solution(mesh):
    placed = (
        P("ens", "tile", None, None, None),
        P("ens", "tile", None, None, None),
        P("tile", None, None),
        P(),
        P(),
        P(),
        P(),
        P(),
        P(),
        P(),
    )
    return jax.shard_map(
        local,
        mesh=mesh,
        in_specs=placed,
        out_specs=(P("ens", "tile", None, None, None), P(), P(), P()),
        check_vma=False,
    )
```

profile of v0, /device:TPU:8, one launch (start us, length us, event | category | flops | bytes accessed | tf_op | source)
XLA Modules:
  0.0 526.0 jit_solution(14262006590394135632)
XLA Ops:
  12.0 1.5 constant_dynamic-slice_fusion.3
  16.0 1.5 fusion.43
  19.4 65.3 %all-gather.5.cloned.1.call-done = bf16[64,1,200,3,128]{4,2,3,1,0:T(8,128)(2,1)} async-done(((bf16[2,1,200,3,128]{4,2,3,1,0:T(8,128)(2,1)}), bf16[64,1,200,3,128]{4,2,3,1,0:T(8,128)(2,1)}) %all-gather.5.cloned.1.call-update) | async-done | bytes 9830416 | tf_op jit(solution)/shard_map/all_gather | solution.py:74
  84.7 9.3 %fusion.39 = (bf16[32,1,1,200,3,128]{5,3,4,2,1,0:T(8,128)(2,1)}, bf16[32,1,1,200,3,128]{5,3,4,2,1,0:T(8,128)(2,1)}) fusion(bf16[32,2,1,200,3,128]{5,3,4,2,1,0:T(8,128)(2,1)} %bitcast.230), kind=kLoop, calls=%fused_computation.131 | loop fusion | bytes 19660800 | tf_op jit(solution)/shard_map/slice | solution.py:75
  105.3 52.3 %all-gather.7.cloned.1.call-done = bf16[64,1,200,3,14]{2,4,3,1,0:T(8,128)(2,1)} async-done(((bf16[2,1,200,3,14]{2,4,3,1,0:T(8,128)(2,1)}), bf16[64,1,200,3,14]{2,4,3,1,0:T(8,128)(2,1)}) %all-gather.7.cloned.1.call-update) | async-done | bytes 1075216 | tf_op jit(solution)/shard_map/all_gather | solution.py:85
  157.6 28.8 %copy.29 = bf16[64,1,200,3,14]{3,2,4,0,1:T(8,128)(2,1)} copy(bf16[64,1,200,3,14]{2,4,3,1,0:T(8,128)(2,1)} %all-gather.7.cloned.1.call-done) | data formatting | bytes 2150400 | tf_op jit(solution)/shard_map/all_gather | solution.py:85
  186.4 30.0 %fusion.38 = (bf16[32,1,1,200,3,14]{4,3,5,2,1,0:T(8,128)(2,1)}, bf16[32,1,1,200,3,14]{4,3,5,2,1,0:T(8,128)(2,1)}) fusion(bf16[32,2,1,200,3,14]{4,3,5,2,1,0:T(8,128)(2,1)} %bitcast.229), kind=kLoop, calls=%fused_computation.130 | loop fusion | bytes 2150400 | tf_op jit(solution)/shard_map/slice | solution.py:86
  216.3 1.4 select_bitcast_fusion
  218.1 1.8 maximum_convert_fusion
  220.3 11.7 %fusion.37 = (f32[8,128]{1,0:T(8,128)S(1)}, f32[1,200,8,128]{3,1,2,0:T(8,128)S(1)}) fusion(f32[1,200,14,134]{3,1,2,0:T(8,128)S(1)} %maximum_convert_fusion, f32[200]{0:T(256)S(1)} %bitcast.247, f32[200]{0:T(256)S(1)} %bitcast.248, f32[200]{0:T(256)S(1)} %bitcast.250, f32[200]{0:T(256)S(1)} %bitcast.251, f32[200]{0:T(256)S(1)} %bitcast.252, ...), kind=kLoop, calls=%fused_computation.129 | loop fusion | flops 20069376 | bytes 41003296 | tf_op jit(solution)/shard_map/reduce_sum | solution.py:99
  233.4 1.5 fusion.28
  236.1 1.7 fusion.5
  237.8 1.8 fusion.26
  239.6 1.5 fusion.17
  241.1 1.6 fusion.13
  242.7 1.6 multiply_reduce_fusion.49
  244.3 6.1 %multiply_reduce_fusion = (f32[200]{0:T(256)S(1)}, f32[200]{0:T(256)S(1)}, f32[200]{0:T(256)S(1)}, f32[200]{0:T(256)S(1)}, f32[200]{0:T(256)S(1)}, /*index=5*/f3...) fusion(f32[1,200,14,134]{3,1,2,0:T(8,128)S(1)} %maximum_convert, ...), kind=kLoop, calls=%fused_computation.30 | loop fusion | flops 8802800 | bytes 17234784 | tf_op jit(solution)/shard_map/reduce_sum | solution.py:137
  251.3 4.7 multiply_reduce_fusion.18
  256.1 4.6 multiply_reduce_fusion.36
  261.0 76.9 %psum.23 = f32[200,49]{0,1:T(8,128)S(1)} all-reduce(f32[200,49]{0,1:T(8,128)S(1)} %stack.223), channel_id=1, replica_groups=mesh['ens'=8,'tile'=32] {'ens','tile'}, use_global_device_ids=true, to_apply=%region_56.57 | all-reduce | flops 9800 | bytes 78400 | tf_op jit(solution)/shard_map/psum | solution.py:144
  338.5 2.4 add_convert_fusion
  340.9 174.4 %all-reduce.3.cloned.1.call-done = (f32[200,800]{1,0:T(8,128)}, f32[800,200]{0,1:T(8,128)}) async-done(((f32[200,800]{1,0:T(8,128)}, f32[800,200]{0,1:T(8,128)}), (f32[200,800]{1,0:T(8,128)}, f32[800,200]{0,1:T(8,128)})) %all-reduce.3.cloned.1.call-update) | async-done | bytes 1280016 | tf_op jit(solution)/shard_map/psum | solution.py:144
  515.4 2.0 broadcast_multiply_fusion
  517.4 2.0 broadcast_multiply_fusion.1
  (144 shorter events, 17.8 us)
Async XLA Ops:
  7.2 225.3 %copy-start = (bf16[200,800]{1,0:T(8,128)(2,1)S(1)}, bf16[200,800]{1,0:T(8,128)(2,1)}, u32[]{:S(2)}) copy-start(bf16[200,800]{1,0:T(8,128)(2,1)} %param.17) | copy-start | bytes 960004
  7.2 77.5 %all-gather.5.cloned.1.call-start = ((), (), s32[]{:S(2)}) async-start(), calls=%async_computation | async-start | bytes 10137600 | tf_op jit(solution)/shard_map/all_gather | solution.py:74
  8.5 88.6 %copy-start.3 = (bf16[1,200,8,128]{3,1,2,0:T(8,128)(2,1)}, bf16[1,200,8,128]{3,1,2,0:T(8,128)(2,1)S(1)}, u32[]{:S(2)}) copy-start(bf16[1,200,8,128]{3,1,2,0:T(8,128)(2,1)S(1)} %compare_select_fusion.2) | copy-start | bytes 1228804
  9.3 148.2 %all-gather.7.cloned.1.call-start = ((), (), s32[]{:S(2)}) async-start(), calls=%async_computation.1 | async-start | bytes 1622016 | tf_op jit(solution)/shard_map/all_gather | solution.py:85
  97.1 3.5 copy-start.4
  97.4 4.2 copy-start.9
  97.4 5.3 %copy-start.12 = (f32[200]{0:T(256)S(1)}, f32[200]{0:T(256)}, u32[]{:S(2)}) copy-start(f32[200]{0:T(256)} %param.19) | copy-start | bytes 2404
  97.5 5.8 %copy-start.10 = (f32[200,49]{0,1:T(8,128)S(1)}, f32[200,49]{0,1:T(8,128)}, u32[]{:S(2)}) copy-start(f32[200,49]{0,1:T(8,128)} %param.15) | copy-start | bytes 117604
  99.2 416.2 %all-reduce.3.cloned.1.call-start = ((), (), s32[]{:S(2)}) async-start(), calls=%async_computation.2 | async-start | bytes 2867200 | tf_op jit(solution)/shard_map/psum | solution.py:144
  217.8 2.2 copy-start.14
  217.8 2.2 copy-start.15
  217.8 2.2 copy-start.16
  217.8 2.2 copy-start.17
  217.8 2.2 copy-start.18
  217.8 2.2 copy-start.19
  217.8 2.2 copy-start.20
  217.8 2.2 copy-start.21
  217.8 2.2 copy-start.22
  220.3 11.9 %copy-start.13 = (f32[200]{0:T(256)S(1)}, f32[200]{0:T(256)}, u32[]{:S(2)}) copy-start(f32[200]{0:T(256)} %param.16) | copy-start | bytes 2404
  233.3 2.4 copy-start.5
  233.4 2.4 copy-start.8
  233.4 2.4 copy-start.11
  233.4 2.4 copy-start.52
  256.1 4.6 copy-start.7
  (33 other events, 67.5 us)
Sparse Core Ops, SparseCore 0:
  10.4 74.2 all-gather.4
  99.3 58.2 all-gather.6
  256.2 259.1 all-reduce.2
where the time goes:
time: 528 us; the launch traced here: 526 us
  waiting for transfers between devices  292 us (55%)
  local copies, waits for them, and re-layouts  80.3 us (15%)
  blocking collectives  76.9 us (15%)
  other arithmetic  45.9 us (9%)
  between operations  21.6 us (4%)
  matrix products  8.73 us (2%)
    psum x1, waiting for transfers between devices, local(): lax.psum((part_in, part_out, part_kernel), ('ens', 'tile'))  174 us
    psum x1, blocking collectives, local(): lax.psum((part_in, part_out, part_kernel), ('ens', 'tile'))  76.9 us
    all_gather x1, waiting for transfers between devices, local(): pieces = lax.all_gather(row_strips, 'tile', axis=0, tiled=True)  65.3 us
    all_gather x1, waiting for transfers between devices, local(): pieces = lax.all_gather(side_cols, 'tile', axis=0, tiled=True)  52.3 us
    slice x1, local copies, waits for them, and re-layouts, local(): west_part = take_slot(held[0], pieces[:, 1], west_slot)  30 us
    all_gather x1, local copies, waits for them, and re-layouts, local(): pieces = lax.all_gather(side_cols, 'tile', axis=0, tiled=True)  28.8 us
    reduce_sum x3, other arithmetic, local(): jnp.sum(grad_conv * extended[:, :, row_off:row_off + row_count, col_off:c...  15.4 us
    reduce_sum x1, other arithmetic, local(): chan_mean = jnp.mean(conv_out, axis=1, keepdims=True)  11.7 us
  transfers between devices with their start and end apart: 3, of which 3 were waited for; matrix products, arithmetic and copies ran while one was open for 3% of the time, Pallas kernels for 0%

commit v1 on v0

--- a/solution.py
+++ b/solution.py
@@ -141,7 +141,9 @@
                 )
             )
     part_kernel = jnp.stack(kernel_terms, axis=1)
-    sum_in, sum_out, sum_kernel = lax.psum((part_in, part_out, part_kernel), ("ens", "tile"))
+    sum_in, sum_out, sum_kernel = lax.psum(
+        lax.psum((part_in, part_out, part_kernel), "ens"), "tile"
+    )
     return (
         block_out[:, None],
         sum_in / entry_total,

time: 528 us -> 682 us (1.29)
  blocking collectives: 76.9 us -> 184 us
  waiting for transfers between devices: 292 us -> 339 us
    psum x1 -> x2, blocking collectives: 76.9 us -> 184 us  [the longest x1 133 us: local(): lax.psum(lax.psum((part_in, part_out, part_kernel), 'ens'), 'tile')]
    psum x1 -> x2, waiting for transfers between devices: 174 us -> 221 us  [the longest x1 139 us: local(): lax.psum((part_in, part_out, part_kernel), 'ens')]
  transfers between devices with their start and end apart: 3 -> 4, of which waited for: 3 -> 4; matrix products, arithmetic and copies ran while one was open for 3% -> 4% of each run, Pallas kernels for 0% -> 0%
where the time goes in v1:
time: 682 us; the launch traced here: 679 us
  waiting for transfers between devices  339 us (50%)
  blocking collectives  184 us (27%)
  local copies, waits for them, and re-layouts  81.5 us (12%)
  other arithmetic  43.7 us (6%)
  between operations  21.7 us (3%)
  matrix products  9.32 us (1%)
    psum x1, waiting for transfers between devices, local(): lax.psum((part_in, part_out, part_kernel), 'ens')  139 us
    psum x1, blocking collectives, local(): lax.psum(lax.psum((part_in, part_out, part_kernel), 'ens'), 'tile')  133 us
    psum x1, waiting for transfers between devices, local(): lax.psum(lax.psum((part_in, part_out, part_kernel), 'ens'), 'tile')  81.5 us
    all_gather x1, waiting for transfers between devices, local(): pieces = lax.all_gather(row_strips, 'tile', axis=0, tiled=True)  65.3 us
    all_gather x1, waiting for transfers between devices, local(): pieces = lax.all_gather(side_cols, 'tile', axis=0, tiled=True)  52.3 us
    psum x1, blocking collectives, local(): lax.psum((part_in, part_out, part_kernel), 'ens')  50.8 us
    slice x1, local copies, waits for them, and re-layouts, local(): west_part = take_slot(held[0], pieces[:, 1], west_slot)  30 us
    all_gather x1, local copies, waits for them, and re-layouts, local(): pieces = lax.all_gather(side_cols, 'tile', axis=0, tiled=True)  28.8 us
  transfers between devices with their start and end apart: 4, of which 4 were waited for; matrix products, arithmetic and copies ran while one was open for 4% of the time, Pallas kernels for 0%

profile of v1, /device:TPU:8, one launch (start us, length us, event | category | flops | bytes accessed | tf_op | source)
XLA Modules:
  0.0 679.3 jit_solution(15825059955726146211)
XLA Ops:
  12.0 1.5 constant_dynamic-slice_fusion.3
  19.4 65.3 %all-gather.5.cloned.1.call-done = bf16[64,1,200,3,128]{4,2,3,1,0:T(8,128)(2,1)} async-done(((bf16[2,1,200,3,128]{4,2,3,1,0:T(8,128)(2,1)}), bf16[64,1,200,3,128]{4,2,3,1,0:T(8,128)(2,1)}) %all-gather.5.cloned.1.call-update) | async-done | bytes 9830416 | tf_op jit(solution)/shard_map/all_gather | solution.py:74
  84.7 9.3 %fusion.39 = (bf16[32,1,1,200,3,128]{5,3,4,2,1,0:T(8,128)(2,1)}, bf16[32,1,1,200,3,128]{5,3,4,2,1,0:T(8,128)(2,1)}) fusion(bf16[32,2,1,200,3,128]{5,3,4,2,1,0:T(8,128)(2,1)} %bitcast.230), kind=kLoop, calls=%fused_computation.131 | loop fusion | bytes 19660800 | tf_op jit(solution)/shard_map/slice | solution.py:75
  105.3 52.3 %all-gather.7.cloned.1.call-done = bf16[64,1,200,3,14]{2,4,3,1,0:T(8,128)(2,1)} async-done(((bf16[2,1,200,3,14]{2,4,3,1,0:T(8,128)(2,1)}), bf16[64,1,200,3,14]{2,4,3,1,0:T(8,128)(2,1)}) %all-gather.7.cloned.1.call-update) | async-done | bytes 1075216 | tf_op jit(solution)/shard_map/all_gather | solution.py:85
  157.6 28.8 %copy.29 = bf16[64,1,200,3,14]{3,2,4,0,1:T(8,128)(2,1)} copy(bf16[64,1,200,3,14]{2,4,3,1,0:T(8,128)(2,1)} %all-gather.7.cloned.1.call-done) | data formatting | bytes 2150400 | tf_op jit(solution)/shard_map/all_gather | solution.py:85
  186.4 30.0 %fusion.38 = (bf16[32,1,1,200,3,14]{4,3,5,2,1,0:T(8,128)(2,1)}, bf16[32,1,1,200,3,14]{4,3,5,2,1,0:T(8,128)(2,1)}) fusion(bf16[32,2,1,200,3,14]{4,3,5,2,1,0:T(8,128)(2,1)} %bitcast.229), kind=kLoop, calls=%fused_computation.130 | loop fusion | bytes 2150400 | tf_op jit(solution)/shard_map/slice | solution.py:86
  218.1 1.8 maximum_convert_fusion
  220.3 11.7 %fusion.37 = (f32[8,128]{1,0:T(8,128)S(1)}, f32[1,200,8,128]{3,1,2,0:T(8,128)S(1)}) fusion(f32[1,200,14,134]{3,1,2,0:T(8,128)S(1)} %maximum_convert_fusion, f32[200]{0:T(256)S(1)} %bitcast.247, f32[200]{0:T(256)S(1)} %bitcast.248, f32[200]{0:T(256)S(1)} %bitcast.250, f32[200]{0:T(256)S(1)} %bitcast.251, f32[200]{0:T(256)S(1)} %bitcast.252, ...), kind=kLoop, calls=%fused_computation.129 | loop fusion | flops 20069376 | bytes 41003296 | tf_op jit(solution)/shard_map/reduce_sum | solution.py:99
  233.4 1.5 fusion.28
  236.1 1.7 fusion.5
  237.8 1.8 fusion.26
  239.6 1.6 fusion.13
  241.2 2.2 copy.34
  243.7 2.1 fusion.17
  246.0 5.3 multiply_reduce_fusion
  251.3 139.2 %all-reduce.7.cloned.1.call-done = (f32[200,800]{1,0:T(8,128)}, f32[800,200]{0,1:T(8,128)}) async-done(((f32[200,800]{1,0:T(8,128)}, f32[800,200]{0,1:T(8,128)}), (f32[200,800]{1,0:T(8,128)}, f32[800,200]{0,1:T(8,128)})) %all-reduce.7.cloned.1.call-update) | async-done | bytes 1280016 | tf_op jit(solution)/shard_map/psum | solution.py:145
  390.6 4.6 multiply_reduce_fusion.36
  395.2 4.7 multiply_reduce_fusion.18
  400.0 50.8 %psum.46 = f32[200,49]{0,1:T(8,128)S(1)} all-reduce(f32[200,49]{0,1:T(8,128)S(1)} %stack.223), channel_id=1, replica_groups=mesh['ens'=8,'tile'=32] {'ens'}, use_global_device_ids=true, to_apply=%region_58.59 | all-reduce | flops 9800 | bytes 78400 | tf_op jit(solution)/shard_map/psum | solution.py:145
  450.8 133.3 %psum.47 = f32[200,49]{0,1:T(8,128)S(1)} all-reduce(f32[200,49]{0,1:T(8,128)S(1)} %psum.46), channel_id=1, replica_groups=mesh['ens'=8,'tile'=32] {'tile'}, use_global_device_ids=true, to_apply=%region_59.60 | all-reduce | flops 9800 | bytes 78400 | tf_op jit(solution)/shard_map/psum | solution.py:144
  584.7 2.5 add_convert_fusion
  587.2 81.5 %all-reduce.5.cloned.1.call-done = (f32[200,800]{1,0:T(8,128)}, f32[800,200]{0,1:T(8,128)}) async-done(((f32[200,800]{1,0:T(8,128)}, f32[800,200]{0,1:T(8,128)}), (f32[200,800]{1,0:T(8,128)}, f32[800,200]{0,1:T(8,128)})) %all-reduce.5.cloned.1.call-update) | async-done | bytes 1280016 | tf_op jit(solution)/shard_map/psum | solution.py:144
  668.7 2.0 broadcast_multiply_fusion
  670.8 2.0 broadcast_multiply_fusion.1
  (150 shorter events, 20.1 us)
Async XLA Ops:
  7.2 225.3 %copy-start = (bf16[200,800]{1,0:T(8,128)(2,1)S(1)}, bf16[200,800]{1,0:T(8,128)(2,1)}, u32[]{:S(2)}) copy-start(bf16[200,800]{1,0:T(8,128)(2,1)} %param.17) | copy-start | bytes 960004
  7.2 77.5 %all-gather.5.cloned.1.call-start = ((), (), s32[]{:S(2)}) async-start(), calls=%async_computation | async-start | bytes 10137600 | tf_op jit(solution)/shard_map/all_gather | solution.py:74
  8.5 88.6 %copy-start.4 = (bf16[1,200,8,128]{3,1,2,0:T(8,128)(2,1)}, bf16[1,200,8,128]{3,1,2,0:T(8,128)(2,1)S(1)}, u32[]{:S(2)}) copy-start(bf16[1,200,8,128]{3,1,2,0:T(8,128)(2,1)S(1)} %compare_select_fusion.2) | copy-start | bytes 1228804
  9.3 148.2 %all-gather.7.cloned.1.call-start = ((), (), s32[]{:S(2)}) async-start(), calls=%async_computation.1 | async-start | bytes 1622016 | tf_op jit(solution)/shard_map/all_gather | solution.py:85
  97.1 3.5 copy-start.5
  97.4 4.2 copy-start.10
  97.4 5.3 copy-start.13
  97.5 5.8 copy-start.11
  99.2 291.4 %all-reduce.7.cloned.1.call-start = ((), (), s32[]{:S(2)}) async-start(), calls=%async_computation.3 | async-start | bytes 2867200 | tf_op jit(solution)/shard_map/psum | solution.py:145
  217.8 2.2 copy-start.15
  217.8 2.2 copy-start.16
  217.8 2.2 copy-start.17
  217.8 2.2 copy-start.18
  217.8 2.2 copy-start.19
  217.8 2.2 copy-start.20
  217.8 2.2 copy-start.21
  217.8 2.2 copy-start.22
  220.3 11.9 %copy-start.14 = (f32[200]{0:T(256)S(1)}, f32[200]{0:T(256)}, u32[]{:S(2)}) copy-start(f32[200]{0:T(256)} %param.16) | copy-start | bytes 2404
  233.3 2.4 copy-start.6
  233.4 2.4 copy-start.9
  233.4 2.4 copy-start.12
  233.4 2.4 copy-start.53
  243.4 425.3 %all-reduce.5.cloned.1.call-start = ((), (), s32[]{:S(2)}) async-start(), calls=%async_computation.2 | async-start | bytes 2867200 | tf_op jit(solution)/shard_map/psum | solution.py:144
  390.6 4.6 copy-start.3
  (35 other events, 72.7 us)
Sparse Core Ops, SparseCore 0:
  10.4 74.2 all-gather.4
  99.3 58.2 all-gather.6
  243.5 146.9 all-reduce.6
  393.1 275.5 all-reduce.4
